TPU v7x, 32 devices: a whole 2x2x4 slice. The times are simulated.
32 devices in a mesh: group: 2 (over y), wide: 8 (over z, x), narrow: 2 (over core).
Axes of the slice: x: 2, y: 2, z: 4, core: 2. Of those that a mesh axis runs over, the one named last changes fastest.
Arguments:
- hidden_in: bfloat16 [16, 16384], P(('group', 'wide'), 'narrow'), parts along dimension 0, may hold values from -60 to 60
- norm_gain: float32 [16384], P('narrow'), may hold values from 0.1 to 1.9
- qkv_weight: bfloat16 [16384, 9216], P('narrow', 'wide'), may hold values from -0.046875 to 0.046875
- out_weight: bfloat16 [8192, 16384], P('narrow', 'wide'), may hold values from -0.25 to 0.25
- cache_keys: bfloat16 [16, 256, 512], P(('group', 'wide'), None, 'narrow'), parts along dimension 0, may hold values from -500 to 500
- cache_values: bfloat16 [16, 256, 512], P(('group', 'wide'), None, 'narrow'), parts along dimension 0, may hold values from -6 to 6
- cache_lengths: int32 [16], P(('group', 'wide')), parts along dimension 0, may hold values from 4 to 256, as said below
Outputs:
- layer_out: float32 [16, 16384], P(('group', 'wide'), 'narrow'), parts along dimension 0
There are 2 independent parts, one for each index of `group`. A program takes and returns all parts, laid end to end along the dimension named above; an argument that names none is the same for every part. Nothing has to cross between parts.
Inputs may be any that keep to these rules, and one draw needn't show every extreme that they name: Some row's length is exactly 256 in every draw; row r's cached positions are 0 to cache_lengths[r] - 1 and its new token stands at position cache_lengths[r].
All inputs are finite; a program needn't handle non-finite values.
Results may differ from a plain program's by a relative error of at most 0.0058.
Values may be sent and summed in bfloat16 or wider, within the bound.
No kernel may reach another device: no remote copies, remote signals or barrier semaphores. Data moves between devices by JAX's collectives and lax.ppermute only.
A program may use at most 64 MiB of HBM per device.

v0:
```python
import jax
import jax.numpy as jnp
from jax import lax
from jax.sharding import PartitionSpec as P

D = 16384
HD = 128
rope_theta = 500000.0
norm_eps = 1e-05


def rotary(values, position):
    half = values.shape[-1] // 2
    frequency = rope_theta ** (-jnp.arange(half, dtype=jnp.float32) * 2.0 / values.shape[-1])
    angles = position[..., None] * frequency
    cosine = jnp.cos(angles)
    sine = jnp.sin(angles)
    first = values[..., :half]
    second = values[..., half:]
    return jnp.concatenate([first * cosine - second * sine, second * cosine + first * sine], -1)


def attend(joined, keys, values, lengths):
    count = joined.shape[0]
    groups = joined.shape[1]
    share = joined.shape[2] - 2
    head_dim = joined.shape[3]
    capacity = keys.shape[1]
    position = lengths.astype(jnp.float32)
    query = (rotary(joined[:, :, :share], position[:, None, None]) * head_dim ** (-0.5)).astype(
        jnp.bfloat16
    )
    new_key = rotary(joined[:, :, share], position[:, None]).astype(jnp.bfloat16)
    new_value = joined[:, :, share + 1].astype(jnp.bfloat16)
    keys_four = keys.reshape(count, capacity, groups, head_dim)
    values_four = values.reshape(count, capacity, groups, head_dim)
    scores = jnp.einsum("bgjd,btgd->bgjt", query, keys_four, preferred_element_type=jnp.float32)
    own = jnp.sum(query.astype(jnp.float32) * new_key.astype(jnp.float32)[:, :, None, :], -1)
    live = jnp.arange(capacity)[None, None, None, :] < lengths[:, None, None, None]
    scores = jnp.where(live, scores, -1e30)
    top = jnp.maximum(jnp.max(scores, -1), own)
    expo = jnp.exp(scores - top[..., None])
    own_expo = jnp.exp(own - top)
    total = jnp.sum(expo, -1) + own_expo
    probs = (expo / total[..., None]).astype(jnp.bfloat16)
    mixed = jnp.einsum("bgjt,btgd->bgjd", probs, values_four, preferred_element_type=jnp.float32)
    mixed = mixed + (own_expo / total)[..., None] * new_value.astype(jnp.float32)[:, :, None, :]
    return mixed.astype(jnp.bfloat16).reshape(count, groups * share * head_dim)


def body(hidden_in, norm_gain, qkv_weight, out_weight, cache_keys, cache_values, cache_lengths):
    inputs = hidden_in.astype(jnp.float32)
    row_count = hidden_in.shape[0]
    squares = lax.psum(jnp.sum(inputs * inputs, -1), "narrow")
    normed = (inputs * lax.rsqrt(squares / D + norm_eps)[:, None] * norm_gain).astype(jnp.bfloat16)
    partial_qkv = jnp.dot(
        lax.all_gather(normed, "wide", axis=0, tiled=True),
        qkv_weight,
        preferred_element_type=jnp.float32,
    )
    all_rows, col_block = partial_qkv.shape
    halves = partial_qkv.reshape(all_rows, 1, 2, col_block // 2)
    paired = lax.psum_scatter(halves, "narrow", scatter_dimension=2, tiled=True)
    moved = lax.all_to_all(paired, "wide", split_axis=0, concat_axis=1, tiled=True)
    blocks = moved.shape[1]
    parted = moved.reshape(row_count, 2, blocks // 2, 1, col_block // 2)
    owned = lax.all_to_all(parted, "narrow", split_axis=1, concat_axis=3, tiled=True)
    owned = owned.reshape(row_count, blocks // 2 * col_block)
    groups = cache_keys.shape[2] // HD
    owned = owned.reshape(row_count, groups, owned.shape[1] // (groups * HD), HD)
    mixed = attend(owned, cache_keys, cache_values, cache_lengths)
    partial_out = jnp.dot(
        lax.all_gather(mixed, "wide", axis=0, tiled=True),
        out_weight,
        preferred_element_type=jnp.float32,
    )
    all_rows, col_block = partial_out.shape
    halves = partial_out.reshape(all_rows, 1, 2, col_block // 2)
    paired = lax.psum_scatter(halves, "narrow", scatter_dimension=2, tiled=True)
    moved = lax.all_to_all(paired, "wide", split_axis=0, concat_axis=1, tiled=True)
    blocks = moved.shape[1]
    parted = moved.reshape(row_count, 2, blocks // 2, 1, col_block // 2)
    added = lax.all_to_all(parted, "narrow", split_axis=1, concat_axis=3, tiled=True)
    added = added.reshape(row_count, blocks // 2 * col_block)
    return inputs + added


def solution(mesh):
    placed = (
        P(("group", "wide"), "narrow"),
        P("narrow"),
        P("narrow", "wide"),
        P("narrow", "wide"),
        P(("group", "wide"), None, "narrow"),
        P(("group", "wide"), None, "narrow"),
        P(("group", "wide")),
    )
    return jax.shard_map(
        body, mesh=mesh, in_specs=placed, out_specs=P(("group", "wide"), "narrow"), check_vma=False
    )
```

profile of v0, /device:TPU:0, one launch (start us, length us, event | category | flops | bytes accessed | tf_op | source)
XLA Modules:
  0.0 149.4 jit_solution(13513085413637469094)
XLA Ops:
  6.5 0.0 copy-start.1
  6.5 0.0 copy-start.2
  6.5 0.0 reduce-scatter.8.cloned.1.call-start
  6.5 1.5 multiply_reduce_fusion
  8.0 3.2 %psum.7 = f32[1]{0:T(128)} all-reduce(f32[1]{0:T(128)} %bitcast.1), channel_id=1, replica_groups=mesh['group'=2,'wide'=8,'narrow'=2] {'narrow'}, use_global_device_ids=true, to_apply=%region_1.0 | all-reduce | flops 1 | bytes 8 | tf_op jit(solution)/shard_map/psum | solution.py:54
  11.9 0.8 convert_bitcast_fusion
  12.8 32.4 %all-gather = bf16[8,1,8192]{2,1,0:T(2,128)(2,1)S(1)} all-gather(bf16[1,1,8192]{2,1,0:T(2,128)(2,1)S(1)} %convert_bitcast_fusion), channel_id=1, replica_groups=mesh['group'=2,'wide'=8,'narrow'=2] {'wide'}, dimensions={0}, use_global_device_ids=true | all-gather | bytes 147456 | tf_op jit(solution)/shard_map/all_gather | solution.py:57
  45.2 7.7 %fusion.1 = f32[8,1152]{1,0:T(8,128)S(1)} fusion(bf16[8192,1152]{1,0:T(8,128)(2,1)} %param.9, bf16[8,1,8192]{2,1,0:T(2,128)(2,1)S(1)} %all-gather), kind=kOutput, calls=%fused_computation.3 | convolution fusion | flops 150994944 | bytes 19042304 | tf_op jit(solution)/shard_map/dot_general | solution.py:56
  52.9 0.0 copy-start
  52.9 0.1 reshape.240
  53.0 0.6 copy.38
  53.6 0.0 reduce-scatter.8.cloned.1.call-update
  54.3 0.1 fusion.19
  54.3 7.9 %reduce-scatter.8.cloned.1.call-done = f32[8,1,1,576]{3,0,1,2:T(8,128)} async-done(((f32[8,1,2,576]{3,0,1,2:T(8,128)}), f32[8,1,1,576]{3,0,1,2:T(8,128)}) %reduce-scatter.8.cloned.1.call-update) | async-done | bytes 18448
  62.2 1.4 copy.39
  63.6 5.7 %all-to-all-start = ((f32[8,1,1,576]{3,2,1,0:T(1,128)}), f32[8,1,1,576]{3,2,1,0:T(1,128)S(1)}, u32[]{:S(2)}, u32[]{:S(2)}) async-start(f32[8,1,1,576]{3,2,1,0:T(1,128)} %copy.39), calls=%async_computation | async-start | bytes 40960 | tf_op jit(solution)/shard_map/all_to_all | solution.py:64
  69.3 0.0 reduce-scatter.6.cloned.1.call-start
  69.3 0.0 copy-done.1
  69.4 0.0 copy-done.2
  69.4 6.4 %all-to-all-done = f32[8,1,1,576]{3,2,1,0:T(1,128)S(1)} async-done(((f32[8,1,1,576]{3,2,1,0:T(1,128)}), f32[8,1,1,576]{3,2,1,0:T(1,128)S(1)}, u32[]{:S(2)}, u32[]{:S(2)}) %all-to-all-start) | async-done | bytes 18464 | tf_op jit(solution)/shard_map/all_to_all | solution.py:64
  75.9 3.7 %all_to_all.48 = f32[1,2,4,1,576]{4,3,2,0,1:T(1,128)S(1)} all-to-all(f32[1,2,4,1,576]{4,3,2,0,1:T(1,128)S(1)} %bitcast.47), channel_id=1, replica_groups=mesh['group'=2,'wide'=8,'narrow'=2] {'narrow'}, dimensions={1} | all-to-all | bytes 36864 | tf_op jit(solution)/shard_map/all_to_all | solution.py:67
  79.6 0.1 reshape_reshape.3
  79.7 0.1 multiply_subtract_fusion
  79.8 0.1 fusion.17
  79.9 0.1 maximum_convert_fusion
  79.9 0.2 multiply_reduce_fusion.1
  80.1 0.3 fusion.25
  80.4 0.2 fusion.9
  80.6 0.2 fusion
  80.8 30.6 %all-gather.1 = bf16[8,1,4096]{2,1,0:T(2,128)(2,1)S(1)} all-gather(bf16[1,1,4096]{2,1,0:T(2,128)(2,1)S(1)} %reshape.251), channel_id=1, replica_groups=mesh['group'=2,'wide'=8,'narrow'=2] {'wide'}, dimensions={0}, use_global_device_ids=true | all-gather | bytes 73728 | tf_op jit(solution)/shard_map/all_gather | solution.py:73
  111.4 8.7 %fusion.6 = f32[8,2048]{1,0:T(8,128)} fusion(bf16[4096,2048]{1,0:T(8,128)(2,1)} %param.10, bf16[8,1,4096]{2,1,0:T(2,128)(2,1)S(1)} %all-gather.1), kind=kOutput, calls=%fused_computation.8 | convolution fusion | flops 134217728 | bytes 16908288 | tf_op jit(solution)/shard_map/dot_general | solution.py:72
  120.1 0.0 reduce-scatter.6.cloned.1.call-update
  120.1 5.0 %reduce-scatter.6.cloned.1.call-done = f32[8,1,1,1024]{3,0,1,2:T(8,128)} async-done(((f32[8,1,2,1024]{3,0,1,2:T(8,128)}), f32[8,1,1,1024]{3,0,1,2:T(8,128)}) %reduce-scatter.6.cloned.1.call-update) | async-done | bytes 32784 | tf_op jit(solution)/shard_map/reduce_scatter | solution.py:79
  125.1 0.8 copy.45
  125.9 12.2 %all_to_all.49 = f32[8,1,1,1024]{3,2,1,0:T(1,128)S(1)} all-to-all(f32[8,1,1,1024]{3,2,1,0:T(1,128)S(1)} %copy.45), channel_id=1, replica_groups=mesh['group'=2,'wide'=8,'narrow'=2] {'wide'}, dimensions={0} | all-to-all | bytes 65536 | tf_op jit(solution)/shard_map/all_to_all | solution.py:80
  138.1 3.7 %all_to_all.50 = f32[1,2,4,1,1024]{4,2,3,0,1:T(4,128)S(1)} all-to-all(f32[1,2,4,1,1024]{4,2,3,0,1:T(4,128)S(1)} %copy.46), channel_id=1, replica_groups=mesh['group'=2,'wide'=8,'narrow'=2] {'narrow'}, dimensions={1} | all-to-all | bytes 65536 | tf_op jit(solution)/shard_map/all_to_all | solution.py:83
  141.9 0.1 reshape.247
  141.9 0.0 copy-done
  141.9 0.7 convert_add_fusion
  (11 shorter events, 0.2 us)
Async XLA Ops:
  6.5 62.8 %copy-start.1 = (bf16[1,256,256]{2,1,0:T(8,128)(2,1)S(1)}, bf16[1,256,256]{2,1,0:T(8,128)(2,1)}, u32[]{:S(2)}) copy-start(bf16[1,256,256]{2,1,0:T(8,128)(2,1)} %param.11) | copy-start | bytes 393220
  6.5 62.9 %copy-start.2 = (bf16[1,256,256]{2,1,0:T(8,128)(2,1)S(1)}, bf16[1,256,256]{2,1,0:T(8,128)(2,1)}, u32[]{:S(2)}) copy-start(bf16[1,256,256]{2,1,0:T(8,128)(2,1)} %param.12) | copy-start | bytes 393220
  6.5 55.7 %reduce-scatter.8.cloned.1.call-start = ((), (), s32[]{:S(2)}) async-start(), calls=%async_computation.7 | async-start | bytes 61440
  52.9 89.0 %copy-start = (bf16[1,8192]{1,0:T(2,128)(2,1)S(1)}, bf16[1,8192]{1,0:T(2,128)(2,1)}, u32[]{:S(2)}) copy-start(bf16[1,8192]{1,0:T(2,128)(2,1)} %param.7) | copy-start | bytes 49156
  63.6 12.3 %all-to-all-start = ((f32[8,1,1,576]{3,2,1,0:T(1,128)}), f32[8,1,1,576]{3,2,1,0:T(1,128)S(1)}, u32[]{:S(2)}, u32[]{:S(2)}) async-start(f32[8,1,1,576]{3,2,1,0:T(1,128)} %copy.39), calls=%async_computation | async-start | bytes 40960 | tf_op jit(solution)/shard_map/all_to_all | solution.py:64
  69.3 55.8 %reduce-scatter.6.cloned.1.call-start = ((), (), s32[]{:S(2)}) async-start(), calls=%async_computation.6 | async-start | bytes 98304 | tf_op jit(solution)/shard_map/reduce_scatter | solution.py:79
Sparse Core Ops, SparseCore 0:
  53.7 8.4 reduce-scatter.7
  120.2 4.7 reduce-scatter.5
where the time goes:
time: 150 us; the launch traced here: 149 us
  blocking collectives  85.9 us (57%)
  waiting for transfers between devices  19.3 us (13%)
  matrix products  16.9 us (11%)
  between operations  14.8 us (10%)
  starting transfers between devices  5.74 us (4%)
  other arithmetic  3.6 us (2%)
  local copies, waits for them, and re-layouts  3.14 us (2%)
    all_gather x1, blocking collectives, body(): lax.all_gather(normed, 'wide', axis=0, tiled=True)  32.4 us
    all_gather x1, blocking collectives, body(): lax.all_gather(mixed, 'wide', axis=0, tiled=True)  30.6 us
    all_to_all x1, blocking collectives, body(): lax.all_to_all(paired, 'wide', split_axis=0, concat_axis=1, tiled=True)  12.2 us
    dot_general x1, matrix products, body(): jnp.dot(lax.all_gather(mixed, 'wide', axis=0, tiled=True), out_weight, pr...  8.68 us
    unnamed x3, waiting for transfers between devices  7.94 us
    dot_general x1, matrix products, body(): jnp.dot(lax.all_gather(normed, 'wide', axis=0, tiled=True), qkv_weight, p...  7.71 us
    all_to_all x2, blocking collectives, body(): lax.all_to_all(parted, 'narrow', split_axis=1, concat_axis=3, tiled=True)  7.46 us
    all_to_all x1, waiting for transfers between devices, body(): lax.all_to_all(paired, 'wide', split_axis=0, concat_axis=1, tiled=True)  6.45 us
  transfers between devices with their start and end apart: 3, of which 3 were waited for; matrix products, arithmetic and copies ran while one was open for 0% of the time, Pallas kernels for 0%

commit v1 on v0

--- a/solution.py
+++ b/solution.py
@@ -7,6 +7,27 @@
 HD = 128
 rope_theta = 500000.0
 norm_eps = 1e-05
+
+
+def gather_around(x, axis, dim):
+    peers, index, span = (lax.axis_size(axis), lax.axis_index(axis), x.shape[dim])
+    ahead = [(i, (i + 1) % peers) for i in range(peers)]
+    backward = [(i, (i - 1) % peers) for i in range(peers)]
+    whole = jnp.zeros((*x.shape[:dim], peers * span, *x.shape[dim + 1 :]), x.dtype)
+    whole = lax.dynamic_update_slice_in_dim(whole, x, index * span, axis=dim)
+    from_left = from_right = x
+    half = peers // 2
+    for step in range(1, half + 1):
+        from_left = lax.ppermute(from_left, axis, ahead)
+        whole = lax.dynamic_update_slice_in_dim(
+            whole, from_left, (index - step) % peers * span, axis=dim
+        )
+        if step < peers - half:
+            from_right = lax.ppermute(from_right, axis, backward)
+            whole = lax.dynamic_update_slice_in_dim(
+                whole, from_right, (index + step) % peers * span, axis=dim
+            )
+    return whole
 
 
 def rotary(values, position):
@@ -70,9 +91,7 @@
     owned = owned.reshape(row_count, groups, owned.shape[1] // (groups * HD), HD)
     mixed = attend(owned, cache_keys, cache_values, cache_lengths)
     partial_out = jnp.dot(
-        lax.all_gather(mixed, "wide", axis=0, tiled=True),
-        out_weight,
-        preferred_element_type=jnp.float32,
+        gather_around(mixed, "wide", 0), out_weight, preferred_element_type=jnp.float32
     )
     all_rows, col_block = partial_out.shape
     halves = partial_out.reshape(all_rows, 1, 2, col_block // 2)

time: 150 us -> 145 us (0.967)
  blocking collectives: 85.9 us -> 55.3 us
  starting transfers between devices: 5.74 us -> 20 us
  waiting for transfers between devices: 19.3 us -> 29.2 us
  local copies, waits for them, and re-layouts: 3.14 us -> 4.92 us
    all_gather x1 -> x0, blocking collectives: 30.6 us -> none  [body(): lax.all_gather(mixed, 'wide', axis=0, tiled=True)]
    ppermute x0 -> x7, starting transfers between devices: none -> 14.2 us  [the longest x3 13.7 us: gather_around(): from_right = lax.ppermute(from_right, axis, backward)]
    ppermute x0 -> x7, waiting for transfers between devices: none -> 9.91 us  [the longest x4 9.9 us: gather_around(): from_left = lax.ppermute(from_left, axis, ahead)]
    dynamic_update_slice x0 -> x8, local copies, waits for them, and re-layouts: none -> 1.77 us  [the longest x4 0.87 us: gather_around(): lax.dynamic_update_slice_in_dim(whole, from_left, (index - step) % peers...]
  transfers between devices with their start and end apart: 3 -> 10, of which waited for: 3 -> 7; matrix products, arithmetic and copies ran while one was open for 0% -> 1% of each run, Pallas kernels for 0% -> 0%
where the time goes in v1:
time: 145 us
  blocking collectives  55.3 us (38%)
  waiting for transfers between devices  29.2 us (20%)
  starting transfers between devices  20 us (14%)
  matrix products  16.8 us (12%)
  between operations  14.9 us (10%)
  local copies, waits for them, and re-layouts  4.92 us (3%)
  other arithmetic  3.6 us (2%)
    all_gather x1, blocking collectives, body(): lax.all_gather(normed, 'wide', axis=0, tiled=True)  32.4 us
    ppermute x3, starting transfers between devices, gather_around(): from_right = lax.ppermute(from_right, axis, backward)  13.7 us
    all_to_all x1, blocking collectives, body(): lax.all_to_all(paired, 'wide', split_axis=0, concat_axis=1, tiled=True)  12.2 us
    ppermute x4, waiting for transfers between devices, gather_around(): from_left = lax.ppermute(from_left, axis, ahead)  9.9 us
    dot_general x1, matrix products, body(): jnp.dot(gather_around(mixed, 'wide', 0), out_weight, preferred_element_ty...  8.66 us
    unnamed x3, waiting for transfers between devices  7.94 us
    dot_general x1, matrix products, body(): jnp.dot(lax.all_gather(normed, 'wide', axis=0, tiled=True), qkv_weight, p...  7.71 us
    all_to_all x2, blocking collectives, body(): lax.all_to_all(parted, 'narrow', split_axis=1, concat_axis=3, tiled=True)  7.46 us
  transfers between devices with their start and end apart: 10, of which 7 were waited for; matrix products, arithmetic and copies ran while one was open for 1% of the time, Pallas kernels for 0%

profile of v1, /device:TPU:0, one launch (start us, length us, event | category | flops | bytes accessed | tf_op | source)
XLA Modules:
  0.0 144.8 jit_solution(13440198395515562684)
XLA Ops:
  6.5 1.5 %multiply_reduce_fusion = f32[]{:T(128)} fusion(bf16[1,8192]{1,0:T(2,128)(2,1)} %param.7), kind=kLoop, calls=%fused_computation.11 | loop fusion | flops 24575 | bytes 16388 | tf_op jit(solution)/shard_map/reduce_sum | solution.py:75
  8.0 3.2 %psum.7 = f32[1]{0:T(128)} all-reduce(f32[1]{0:T(128)} %bitcast.1), channel_id=1, replica_groups=mesh['group'=2,'wide'=8,'narrow'=2] {'narrow'}, use_global_device_ids=true, to_apply=%region_1.0 | all-reduce | flops 1 | bytes 8 | tf_op jit(solution)/shard_map/psum | solution.py:75
  11.9 0.8 convert_bitcast_fusion
  12.8 32.4 %all-gather = bf16[8,1,8192]{2,1,0:T(2,128)(2,1)S(1)} all-gather(bf16[1,1,8192]{2,1,0:T(2,128)(2,1)S(1)} %convert_bitcast_fusion), channel_id=1, replica_groups=mesh['group'=2,'wide'=8,'narrow'=2] {'wide'}, dimensions={0}, use_global_device_ids=true | all-gather | bytes 147456 | tf_op jit(solution)/shard_map/all_gather | solution.py:78
  45.2 7.7 %fusion.1 = f32[8,1152]{1,0:T(8,128)S(1)} fusion(bf16[8192,1152]{1,0:T(8,128)(2,1)} %param.9, bf16[8,1,8192]{2,1,0:T(2,128)(2,1)S(1)} %all-gather), kind=kOutput, calls=%fused_computation.3 | convolution fusion | flops 150994944 | bytes 19042304 | tf_op jit(solution)/shard_map/dot_general | solution.py:77
  52.9 0.1 reshape.240
  53.0 0.6 copy.36
  53.6 0.0 reduce-scatter.8.cloned.1.call-update
  54.3 0.1 fusion.16
  54.3 7.9 %reduce-scatter.8.cloned.1.call-done = f32[8,1,1,576]{3,0,1,2:T(8,128)} async-done(((f32[8,1,2,576]{3,0,1,2:T(8,128)}), f32[8,1,1,576]{3,0,1,2:T(8,128)}) %reduce-scatter.8.cloned.1.call-update) | async-done | bytes 18448
  62.2 1.4 copy.37
  63.6 5.7 %all-to-all-start = ((f32[8,1,1,576]{3,2,1,0:T(1,128)}), f32[8,1,1,576]{3,2,1,0:T(1,128)S(1)}, u32[]{:S(2)}, u32[]{:S(2)}) async-start(f32[8,1,1,576]{3,2,1,0:T(1,128)} %copy.37), calls=%async_computation | async-start | bytes 40960 | tf_op jit(solution)/shard_map/all_to_all | solution.py:85
  69.3 0.0 reduce-scatter.6.cloned.1.call-start
  69.4 6.4 %all-to-all-done = f32[8,1,1,576]{3,2,1,0:T(1,128)S(1)} async-done(((f32[8,1,1,576]{3,2,1,0:T(1,128)}), f32[8,1,1,576]{3,2,1,0:T(1,128)S(1)}, u32[]{:S(2)}, u32[]{:S(2)}) %all-to-all-start) | async-done | bytes 18464 | tf_op jit(solution)/shard_map/all_to_all | solution.py:85
  75.9 3.7 %all_to_all.48 = f32[1,2,4,1,576]{4,3,2,0,1:T(1,128)S(1)} all-to-all(f32[1,2,4,1,576]{4,3,2,0,1:T(1,128)S(1)} %bitcast.45), channel_id=1, replica_groups=mesh['group'=2,'wide'=8,'narrow'=2] {'narrow'}, dimensions={1} | all-to-all | bytes 36864 | tf_op jit(solution)/shard_map/all_to_all | solution.py:88
  79.6 0.1 reshape_reshape.3
  79.7 0.1 multiply_subtract_fusion
  79.8 0.1 fusion.14
  79.9 0.1 maximum_convert_fusion
  79.9 0.2 multiply_reduce_fusion.1
  80.1 0.3 fusion.22
  80.4 0.2 fusion.6
  80.6 0.2 fusion
  80.8 0.6 collective-permute-start
  81.4 4.2 %collective-permute-start.1 = (bf16[1,4096]{1,0:T(2,128)(2,1)S(1)}, bf16[1,4096]{1,0:T(2,128)(2,1)S(1)}, u32[]{:S(2)}, u32[]{:S(2)}) collective-permute-start(bf16[1,4096]{1,0:T(2,128)(2,1)S(1)} %reshape.244), channel_id=1, source_target_pairs={{0,14},{2,0},{4,2},{6,4},{8,6},{10,8},{12,10},{14,12},{1,15},{3,1}... | collective-permute-start | bytes 24584 | tf_op jit(solution)/shard_map/ppermute | solution.py:26
  85.6 1.7 %collective-permute-done = bf16[1,4096]{1,0:T(2,128)(2,1)S(1)} collective-permute-done((bf16[1,4096]{1,0:T(2,128)(2,1)S(1)}, bf16[1,4096]{1,0:T(2,128)(2,1)S(1)}, u32[]{:S(2)}, u32[]{:S(2)}) %collective-permute-start) | collective-permute-done | bytes 8224 | tf_op jit(solution)/shard_map/ppermute | solution.py:21
  87.3 0.0 collective-permute-done.1
  87.3 4.7 %collective-permute-start.3 = (bf16[1,4096]{1,0:T(2,128)(2,1)S(1)}, bf16[1,4096]{1,0:T(2,128)(2,1)S(1)}, u32[]{:S(2)}, u32[]{:S(2)}) collective-permute-start(bf16[1,4096]{1,0:T(2,128)(2,1)S(1)} %collective-permute-done.1), channel_id=1, source_target_pairs={{0,14},{2,0},{4,2},{6,4},{8,6},{10,8},{12,10},{14,12},{1,15},{3,1}... | collective-permute-start | bytes 24584 | tf_op jit(solution)/shard_map/ppermute | solution.py:26
  92.0 1.7 %collective-permute-done.2 = bf16[1,4096]{1,0:T(2,128)(2,1)S(1)} collective-permute-done((bf16[1,4096]{1,0:T(2,128)(2,1)S(1)}, bf16[1,4096]{1,0:T(2,128)(2,1)S(1)}, u32[]{:S(2)}, u32[]{:S(2)}) %collective-permute-start.2) | collective-permute-done | bytes 8224 | tf_op jit(solution)/shard_map/ppermute | solution.py:21
  93.7 4.7 %collective-permute-start.5 = (bf16[1,4096]{1,0:T(2,128)(2,1)S(1)}, bf16[1,4096]{1,0:T(2,128)(2,1)S(1)}, u32[]{:S(2)}, u32[]{:S(2)}) collective-permute-start(bf16[1,4096]{1,0:T(2,128)(2,1)S(1)} %collective-permute-done.3), channel_id=1, source_target_pairs={{0,14},{2,0},{4,2},{6,4},{8,6},{10,8},{12,10},{14,12},{1,15},{3,1}... | collective-permute-start | bytes 24584 | tf_op jit(solution)/shard_map/ppermute | solution.py:26
  98.5 1.7 %collective-permute-done.4 = bf16[1,4096]{1,0:T(2,128)(2,1)S(1)} collective-permute-done((bf16[1,4096]{1,0:T(2,128)(2,1)S(1)}, bf16[1,4096]{1,0:T(2,128)(2,1)S(1)}, u32[]{:S(2)}, u32[]{:S(2)}) %collective-permute-start.4) | collective-permute-done | bytes 8224 | tf_op jit(solution)/shard_map/ppermute | solution.py:21
  100.2 0.2 dynamic_update_slice.24
  100.4 0.2 dynamic_update_slice.25
  100.6 0.2 dynamic_update_slice.26
  100.9 0.2 dynamic_update_slice.27
  101.1 0.2 dynamic_update_slice.28
  101.3 0.2 dynamic_update_slice.29
  101.6 0.2 dynamic_update_slice.30
  101.8 4.8 %collective-permute-done.6 = bf16[1,4096]{1,0:T(2,128)(2,1)S(1)} collective-permute-done((bf16[1,4096]{1,0:T(2,128)(2,1)S(1)}, bf16[1,4096]{1,0:T(2,128)(2,1)S(1)}, u32[]{:S(2)}, u32[]{:S(2)}) %collective-permute-start.6) | collective-permute-done | bytes 8224 | tf_op jit(solution)/shard_map/ppermute | solution.py:21
  106.6 0.2 dynamic_update_slice.31
  106.8 8.7 %fusion.23 = f32[8,2048]{1,0:T(8,128)} fusion(bf16[8,4096]{1,0:T(8,128)(2,1)S(1)} %dynamic_update_slice.31, bf16[4096,2048]{1,0:T(8,128)(2,1)} %param.10), kind=kOutput, calls=%fused_computation.41 | convolution fusion | flops 134217728 | bytes 16908288 | tf_op jit(solution)/shard_map/dot_general | solution.py:93
  115.5 0.0 reduce-scatter.6.cloned.1.call-update
  115.5 5.0 %reduce-scatter.6.cloned.1.call-done = f32[8,1,1,1024]{3,0,1,2:T(8,128)} async-done(((f32[8,1,2,1024]{3,0,1,2:T(8,128)}), f32[8,1,1,1024]{3,0,1,2:T(8,128)}) %reduce-scatter.6.cloned.1.call-update) | async-done | bytes 32784 | tf_op jit(solution)/shard_map/reduce_scatter | solution.py:98
  120.4 0.8 copy.43
  121.2 12.2 %all_to_all.49 = f32[8,1,1,1024]{3,2,1,0:T(1,128)S(1)} all-to-all(f32[8,1,1,1024]{3,2,1,0:T(1,128)S(1)} %copy.43), channel_id=1, replica_groups=mesh['group'=2,'wide'=8,'narrow'=2] {'wide'}, dimensions={0} | all-to-all | bytes 65536 | tf_op jit(solution)/shard_map/all_to_all | solution.py:99
  133.4 3.7 %all_to_all.50 = f32[1,2,4,1,1024]{4,2,3,0,1:T(4,128)S(1)} all-to-all(f32[1,2,4,1,1024]{4,2,3,0,1:T(4,128)S(1)} %copy.44), channel_id=1, replica_groups=mesh['group'=2,'wide'=8,'narrow'=2] {'narrow'}, dimensions={1} | all-to-all | bytes 65536 | tf_op jit(solution)/shard_map/all_to_all | solution.py:102
  137.2 0.1 reshape.247
  137.3 0.7 convert_add_fusion
  (24 shorter events, 0.2 us)
Async XLA Ops:
  6.5 62.8 %copy-start.1 = (bf16[1,256,256]{2,1,0:T(8,128)(2,1)S(1)}, bf16[1,256,256]{2,1,0:T(8,128)(2,1)}, u32[]{:S(2)}) copy-start(bf16[1,256,256]{2,1,0:T(8,128)(2,1)} %param.11) | copy-start | bytes 393220
  6.5 62.9 %copy-start.2 = (bf16[1,256,256]{2,1,0:T(8,128)(2,1)S(1)}, bf16[1,256,256]{2,1,0:T(8,128)(2,1)}, u32[]{:S(2)}) copy-start(bf16[1,256,256]{2,1,0:T(8,128)(2,1)} %param.12) | copy-start | bytes 393220
  6.5 55.7 %reduce-scatter.8.cloned.1.call-start = ((), (), s32[]{:S(2)}) async-start(), calls=%async_computation.7 | async-start | bytes 61440
  52.9 84.4 %copy-start = (bf16[1,8192]{1,0:T(2,128)(2,1)S(1)}, bf16[1,8192]{1,0:T(2,128)(2,1)}, u32[]{:S(2)}) copy-start(bf16[1,8192]{1,0:T(2,128)(2,1)} %param.7) | copy-start | bytes 49156
  63.6 12.3 %all-to-all-start = ((f32[8,1,1,576]{3,2,1,0:T(1,128)}), f32[8,1,1,576]{3,2,1,0:T(1,128)S(1)}, u32[]{:S(2)}, u32[]{:S(2)}) async-start(f32[8,1,1,576]{3,2,1,0:T(1,128)} %copy.37), calls=%async_computation | async-start | bytes 40960 | tf_op jit(solution)/shard_map/all_to_all | solution.py:85
  69.3 51.1 %reduce-scatter.6.cloned.1.call-start = ((), (), s32[]{:S(2)}) async-start(), calls=%async_computation.6 | async-start | bytes 98304 | tf_op jit(solution)/shard_map/reduce_scatter | solution.py:98
  80.8 6.5 %collective-permute-start = (bf16[1,4096]{1,0:T(2,128)(2,1)S(1)}, bf16[1,4096]{1,0:T(2,128)(2,1)S(1)}, u32[]{:S(2)}, u32[]{:S(2)}) collective-permute-start(bf16[1,4096]{1,0:T(2,128)(2,1)S(1)} %reshape.244), channel_id=1, source_target_pairs={{0,2},{2,4},{4,6},{6,8},{8,10},{10,12},{12,14},{14,0},{1,3},{3,5},... | collective-permute-start | bytes 24584 | tf_op jit(solution)/shard_map/ppermute | solution.py:21
  81.4 5.9 %collective-permute-start.1 = (bf16[1,4096]{1,0:T(2,128)(2,1)S(1)}, bf16[1,4096]{1,0:T(2,128)(2,1)S(1)}, u32[]{:S(2)}, u32[]{:S(2)}) collective-permute-start(bf16[1,4096]{1,0:T(2,128)(2,1)S(1)} %reshape.244), channel_id=1, source_target_pairs={{0,14},{2,0},{4,2},{6,4},{8,6},{10,8},{12,10},{14,12},{1,15},{3,1}... | collective-permute-start | bytes 24584 | tf_op jit(solution)/shard_map/ppermute | solution.py:26
  87.3 6.4 %collective-permute-start.2 = (bf16[1,4096]{1,0:T(2,128)(2,1)S(1)}, bf16[1,4096]{1,0:T(2,128)(2,1)S(1)}, u32[]{:S(2)}, u32[]{:S(2)}) collective-permute-start(bf16[1,4096]{1,0:T(2,128)(2,1)S(1)} %collective-permute-done), channel_id=1, source_target_pairs={{0,2},{2,4},{4,6},{6,8},{8,10},{10,12},{12,14},{14,0},{1,3},{3,5},... | collective-permute-start | bytes 24584 | tf_op jit(solution)/shard_map/ppermute | solution.py:21
  87.3 6.4 %collective-permute-start.3 = (bf16[1,4096]{1,0:T(2,128)(2,1)S(1)}, bf16[1,4096]{1,0:T(2,128)(2,1)S(1)}, u32[]{:S(2)}, u32[]{:S(2)}) collective-permute-start(bf16[1,4096]{1,0:T(2,128)(2,1)S(1)} %collective-permute-done.1), channel_id=1, source_target_pairs={{0,14},{2,0},{4,2},{6,4},{8,6},{10,8},{12,10},{14,12},{1,15},{3,1}... | collective-permute-start | bytes 24584 | tf_op jit(solution)/shard_map/ppermute | solution.py:26
  93.7 6.4 %collective-permute-start.4 = (bf16[1,4096]{1,0:T(2,128)(2,1)S(1)}, bf16[1,4096]{1,0:T(2,128)(2,1)S(1)}, u32[]{:S(2)}, u32[]{:S(2)}) collective-permute-start(bf16[1,4096]{1,0:T(2,128)(2,1)S(1)} %collective-permute-done.2), channel_id=1, source_target_pairs={{0,2},{2,4},{4,6},{6,8},{8,10},{10,12},{12,14},{14,0},{1,3},{3,5},... | collective-permute-start | bytes 24584 | tf_op jit(solution)/shard_map/ppermute | solution.py:21
  93.7 7.9 %collective-permute-start.5 = (bf16[1,4096]{1,0:T(2,128)(2,1)S(1)}, bf16[1,4096]{1,0:T(2,128)(2,1)S(1)}, u32[]{:S(2)}, u32[]{:S(2)}) collective-permute-start(bf16[1,4096]{1,0:T(2,128)(2,1)S(1)} %collective-permute-done.3), channel_id=1, source_target_pairs={{0,14},{2,0},{4,2},{6,4},{8,6},{10,8},{12,10},{14,12},{1,15},{3,1}... | collective-permute-start | bytes 24584 | tf_op jit(solution)/shard_map/ppermute | solution.py:26
  100.2 6.4 %collective-permute-start.6 = (bf16[1,4096]{1,0:T(2,128)(2,1)S(1)}, bf16[1,4096]{1,0:T(2,128)(2,1)S(1)}, u32[]{:S(2)}, u32[]{:S(2)}) collective-permute-start(bf16[1,4096]{1,0:T(2,128)(2,1)S(1)} %collective-permute-done.4), channel_id=1, source_target_pairs={{0,2},{2,4},{4,6},{6,8},{8,10},{10,12},{12,14},{14,0},{1,3},{3,5},... | collective-permute-start | bytes 24584 | tf_op jit(solution)/shard_map/ppermute | solution.py:21
Sparse Core Ops, SparseCore 0:
  53.7 8.4 reduce-scatter.7
  115.6 4.7 reduce-scatter.5
